TPU v7x, 128 devices: a whole 4x4x4 slice. The times are simulated.
128 devices in a mesh: stream: 16 (over y, z), rows: 8 (over x, core).
Axes of the slice: x: 4, y: 4, z: 4, core: 2. Of those that a mesh axis runs over, the one named last changes fastest.
Arguments:
- tracers: float32 [8, 512, 16384], P(None, 'rows', 'stream'), may hold values from -6 to 6
- shifts: int32 [512, 16384], P('rows', 'stream'), may hold values from 0 to 2046, as said below
- fractions: float32 [512, 16384], P('rows', 'stream'), may hold values from 0 to 1
- record_owner: int32 [8, 256, 1], P('rows', 'stream'), may hold values from 0 to 15; in each aligned block of 16 rows (0 to 15, 16 to 31, ..., all dimensions but the last counted through in order) at most 2 rows name the same one
- record_source: int32 [8, 256], P('rows', 'stream'), may hold values from 0 to 15
- record_parity: int32 [8, 256], P('rows', 'stream'), may hold values from 0 to 1
- record_place: int32 [8, 256], P('rows', 'stream'), may hold values from 0 to 31
Outputs:
- tracers_out: float32 [8, 512, 16384], P(None, 'rows', 'stream')
Inputs may be any that keep to these rules, and one draw needn't show every extreme that they name: Along one row the shifts lie within five consecutive values; the largest is reached in every draw. `record_owner`: among the 16 records of one device at most 2 name the same owner.
All inputs are finite; a program needn't handle non-finite values.
Results may differ from a plain program's by a relative error of at most 0.0003.
Values sent between devices are 32-bit elements; how exact they have to be, the bound alone decides.
A program may use at most 128 MiB of HBM per device.

v0:
```python
import jax
import jax.numpy as jnp
from jax import lax
from jax.experimental import pallas as pl
from jax.experimental.pallas import tpu as pltpu
from jax.sharding import PartitionSpec as P

BLOCK = 64
ROWS = 64
COLS = 1024
TR = 8
LANES = 128
TILES = COLS // LANES
PAD = 2
OWN = PAD + 2 * TILES
WIDTH = OWN + TILES + 1
CHUNKS = 8
CR = ROWS // CHUNKS
FORWARD = 5
MESH = pl.DeviceIdType.MESH
HIGHEST = lax.Precision.HIGHEST


def shifted(pieces, amount):
    if amount == 0:
        return pieces[:-1]
    lane = lax.broadcasted_iota(jnp.int32, (TR, LANES), 1)
    turned = [pltpu.roll(piece, LANES - amount, 1) for piece in pieces]
    return [
        jnp.where(lane < LANES - amount, turned[i], turned[i + 1]) for i in range(len(pieces) - 1)
    ]


def sweep_kernel(
    t_ref, shift_ref, frac_ref, owner_in, source_in, parity_in, place_in,
    out_ref,
    owner_ref, source_ref, parity_ref, place_ref, own_buf, near_buf, far_buf, work, relay_buf, shift_tile, frac_tile, least_v, least_s, lhs, ones_mat, faces,
    hot_a, hot_b, codes, send_buf, recv_buf,
    own_sem, tile_sem, record_sem, edge_send, edge_recv, least_sem,
    first_send, first_recv, middle_send, middle_recv, last_send, last_recv, msg_send, msg_recv, msg_own,
):
    s = lax.axis_index("stream")
    row = lax.axis_index("rows")
    y, z = s // 4, s % 4
    partner = row + 1 - 2 * (row % 2)
    after = ((s + 1) % 16, row)
    ahead = ((s + 15) % 16, row)
    via = (((y + jnp.where(z == 2, 1, 0)) % 4) * 4 + (z + 3) % 4, row)
    from_z = (z + 1) % 4
    from_s = ((y + jnp.where(from_z == 2, 3, 0)) % 4) * 4 + from_z
    relayed_to = ((from_s + 2) % 16, row)

    barrier = pltpu.get_barrier_semaphore()

    def greet(step, carry):
        other = (s + step) % 16
        pl.semaphore_signal(barrier, inc=1, device_id=(other, row), device_id_type=MESH)
        pl.semaphore_signal(barrier, inc=1, device_id=(other, partner), device_id_type=MESH)
        return carry

    lax.fori_loop(1, 16, greet, 0)
    pl.semaphore_signal(barrier, inc=1, device_id=(s, partner), device_id_type=MESH)
    own_copy = pltpu.make_async_copy(t_ref, own_buf, own_sem)
    own_copy.start()
    staged = [
        pltpu.make_async_copy(source, target, record_sem.at[i])
        for i, (source, target) in enumerate(
            [(owner_in, owner_ref), (source_in, source_ref), (parity_in, parity_ref), (place_in, place_ref)])
    ] + [
        pltpu.make_async_copy(source.at[:, pl.ds(j * LANES, LANES)], target.at[j + 1], tile_sem.at[i, j])
        for i, (source, target) in enumerate([(shift_ref, shift_tile), (frac_ref, frac_tile)])
        for j in range(TILES)
    ]
    for copy in staged:
        copy.start()
    pl.semaphore_wait(barrier, 31)

    def unit(ref, c):
        return ref.at[:, c]

    def direct(c):
        return pltpu.make_async_remote_copy(
            unit(t_ref, c), unit(near_buf, c),
            first_send.at[c], first_recv.at[c], device_id=after, device_id_type=MESH)

    def forward(c):
        return pltpu.make_async_remote_copy(
            unit(near_buf, c), unit(far_buf, c),
            last_send.at[c], last_recv.at[c], device_id=after, device_id_type=MESH)

    def leg_1(c):
        return pltpu.make_async_remote_copy(
            unit(t_ref, c), unit(relay_buf, c - FORWARD),
            first_send.at[c], first_recv.at[c], device_id=via, device_id_type=MESH)

    def leg_2(c):
        return pltpu.make_async_remote_copy(
            unit(relay_buf, c - FORWARD), unit(far_buf, c),
            middle_send.at[c - FORWARD], middle_recv.at[c - FORWARD],
            device_id=relayed_to, device_id_type=MESH)

    def leg_3(c):
        return pltpu.make_async_remote_copy(
            unit(far_buf, c), unit(near_buf, c),
            last_send.at[c], last_recv.at[c], device_id=ahead, device_id_type=MESH)

    tail = pl.ds(COLS - LANES, LANES)
    edge_s = pltpu.make_async_remote_copy(
        shift_ref.at[:, tail], shift_tile.at[0], edge_send.at[0], edge_recv.at[0],
        device_id=after, device_id_type=MESH)
    edge_f = pltpu.make_async_remote_copy(
        frac_ref.at[:, tail], frac_tile.at[0], edge_send.at[1], edge_recv.at[1],
        device_id=after, device_id_type=MESH)
    edge_s.start()
    edge_f.start()
    direct(0).start()
    leg_1(FORWARD).start()
    direct(1).start()
    leg_1(FORWARD + 1).start()

    lane = lax.broadcasted_iota(jnp.int32, (TR, LANES), 1)
    zero = jnp.zeros((CR, TR, LANES), jnp.float32)
    work[0] = zero
    work[1] = zero
    work[WIDTH - 1] = zero
    cell = lax.broadcasted_iota(jnp.int32, (COLS, LANES), 0)
    face = lax.broadcasted_iota(jnp.int32, (COLS, LANES), 1)
    ones_mat[0:COLS, :] = jnp.where(cell < face * BLOCK, 1.0, 0.0)
    ones_mat[COLS:, :] = jnp.ones((LANES, LANES), jnp.float32)

    for copy in staged:
        copy.wait()
    slot = lax.broadcasted_iota(jnp.int32, (LANES, LANES), 0)
    column = lax.broadcasted_iota(jnp.int32, (LANES, LANES), 1)
    first_hot = jnp.zeros((LANES, LANES), jnp.float32)
    second_hot = first_hot
    code = first_hot
    for j in range(16):
        owner = owner_ref[0, j]
        earlier = jnp.int32(0)
        for i in range(j):
            earlier = earlier + jnp.where(owner_ref[0, i] == owner, 1, 0)
        at = owner * 8 + 2 * earlier
        here = column == source_ref[0, j] + 1
        label = (parity_ref[0, j] * 32 + place_ref[0, j] + 1).astype(jnp.float32)
        first_hot = jnp.where((slot == at) & here, 1.0, first_hot)
        second_hot = jnp.where((slot == at + 1) & here, 1.0, second_hot)
        code = jnp.where((slot == at + 4) | (slot == at + 5), label, code)
    hot_a[...] = first_hot
    hot_b[...] = second_hot
    codes[...] = code

    edge_s.wait_recv()
    edge_f.wait_recv()
    least = jnp.min(jnp.min(shift_tile[...], axis=0), axis=1, keepdims=True)
    least_v[...] = jnp.broadcast_to(least, (ROWS, LANES))
    least_copy = pltpu.make_async_copy(least_v, least_s, least_sem)
    least_copy.start()

    def one_row(local, c):
        r = c * CR + local
        low = least_s[r, 0]
        start = OWN * LANES - LANES - 5 - low
        tile = start // LANES
        turn = start % LANES
        piece = []
        for j in range(11):
            piece.append(pltpu.roll(work[tile + j, local], (LANES - turn) % LANES, 1))
        moved = [jnp.where(lane < LANES - turn, piece[j], piece[j + 1]) for j in range(10)]
        cells = [shifted(moved, 5 - i) for i in range(6)]
        gains = []
        for j in range(9):
            n = shift_tile[j, pl.ds(r, TR, stride=0), :]
            f = frac_tile[j, pl.ds(r, TR, stride=0), :]
            offset = n - low
            upwind = cells[0][j]
            before = cells[1][j]
            passed = jnp.zeros((TR, LANES), jnp.float32)
            total = passed
            for step in range(1, 5):
                total = total + cells[step - 1][j]
                hit = offset == step
                upwind = jnp.where(hit, cells[step][j], upwind)
                before = jnp.where(hit, cells[step + 1][j], before)
                passed = jnp.where(hit, total, passed)
            gains.append(passed + f * upwind + (upwind - before) * (f * (1.0 - f) * 0.5))
        back = [pltpu.roll(gain, 1, 1) for gain in gains]
        at_lhs = pl.ds(pl.multiple_of(local * TR, TR), TR)
        for j in range(1, 9):
            advected = cells[0][j] + jnp.where(lane == 0, back[j - 1], back[j]) - gains[j]
            out_ref[r, :, (j - 1) * LANES : j * LANES] = advected
            own = work[OWN + j - 1, local]
            lhs[at_lhs, pl.ds((j - 1) * LANES, LANES)] = own - advected
        whole = jnp.where(lane == LANES - 1, gains[0], 0.0)
        for j in range(PAD, OWN):
            reached = lane >= (OWN - j) * LANES - low
            whole = whole + jnp.where(reached, work[j, local], 0.0)
        lhs[at_lhs, pl.ds(COLS, LANES)] = whole
        return c

    def finish(c):
        forward(c).wait_recv()
        for j in range(TILES):
            work[PAD + j] = jnp.where(s >= 2, jnp.transpose(far_buf[:, c, j], (1, 0, 2)), 0.0)
            work[PAD + TILES + j] = jnp.where(
                s >= 1, jnp.transpose(near_buf[:, c, j], (1, 0, 2)), 0.0)
            work[OWN + j] = jnp.transpose(own_buf[:, c, j], (1, 0, 2))
        lax.fori_loop(0, CR, one_row, c, unroll=4)
        faces[pl.ds(pl.multiple_of(c * CR * TR, CR * TR), CR * TR), :] = jnp.dot(
            lhs[...], ones_mat[...], precision=HIGHEST, preferred_element_type=jnp.float32)

    def pass_on(c):
        direct(c).wait_recv()
        forward(c).start()

    def first_on(c):
        leg_1(c).wait_recv()
        leg_2(c).start()

    def second_on(c):
        leg_2(c).wait_recv()
        leg_3(c).start()

    def next_direct(c):
        direct(c).wait_send()
        direct(c + 2).start()

    pass_on(0)
    next_direct(0)
    first_on(5)
    leg_1(5).wait_send()
    leg_1(7).start()
    pass_on(1)
    next_direct(1)
    first_on(6)
    second_on(5)
    own_copy.wait()
    least_copy.wait()
    pass_on(2)
    next_direct(2)
    first_on(7)
    second_on(6)
    finish(0)
    pass_on(3)
    second_on(7)
    finish(1)
    finish(5)
    pass_on(4)
    finish(2)
    finish(6)
    finish(3)
    finish(7)
    finish(4)

    pairs = faces[...].reshape(ROWS // 2, 2, TR, LANES)
    fine = (0.5 * (pairs[:, 0] + pairs[:, 1])).reshape(ROWS // 2 * TR, LANES)
    across = (((1,), (1,)), ((), ()))
    half = ROWS // 4 * TR
    packed = (
        lax.dot_general(hot_a[...], fine[:half], across, precision=HIGHEST,
                        preferred_element_type=jnp.float32)
        + lax.dot_general(hot_b[...], fine[half:], across, precision=HIGHEST,
                          preferred_element_type=jnp.float32)
        + codes[...]
    )
    send_buf[...] = packed.reshape(16, 8, LANES)

    def message(other, other_row, slot_base, k):
        return pltpu.make_async_remote_copy(
            send_buf.at[other], recv_buf.at[slot_base + s], msg_send.at[k], msg_recv,
            device_id=(other, other_row), device_id_type=MESH)

    to_self = pltpu.make_async_copy(send_buf.at[s], recv_buf.at[s], msg_recv)
    to_self.start()
    message(s, partner, 16, 0).start()

    def send_out(step, carry):
        other = (s + step) % 16
        message(other, row, 0, 2 * step).start()
        message(other, partner, 16, 2 * step + 1).start()
        return carry

    lax.fori_loop(1, 16, send_out, 0)

    for c in range(CHUNKS):
        forward(c).wait_send()
    for c in (3, 4):
        direct(c).wait_send()
    for c in (5, 6, 7):
        if c != 5:
            leg_1(c).wait_send()
        leg_2(c).wait_send()
    edge_s.wait_send()
    edge_f.wait_send()

    pltpu.make_async_copy(recv_buf, recv_buf, msg_recv).wait()

    received = recv_buf[...]
    names = pltpu.roll(received, 4, 1).reshape(2 * LANES, LANES)
    received = received.reshape(2 * LANES, LANES)
    part = lax.broadcasted_iota(jnp.int32, (2 * LANES, LANES), 0) % 8
    spot = lax.broadcasted_iota(jnp.int32, (2 * LANES, LANES), 1)
    down = (((0,), (0,)), ((), ()))
    sums = []
    counts = []
    for side in range(2):
        wanted = jnp.where(spot < 16, (row % 2) * 32 + 2 * spot + side + 1, -1).astype(jnp.float32)
        found = names == wanted
        for h in range(2):
            hot = jnp.where(found & ((part == h) | (part == h + 2)), 1.0, 0.0)
            sums.append(lax.dot_general(received, hot, down, precision=HIGHEST,
                                        preferred_element_type=jnp.float32))
            if h == 0:
                counts.append(jnp.dot(jnp.ones((8, 2 * LANES), jnp.float32), hot,
                                      preferred_element_type=jnp.float32))
    for side in range(2):
        for h in range(2):
            lhs[0:LANES // 2, (side * 4 + h * 2) * LANES:(side * 4 + h * 2 + 1) * LANES] = (
                sums[side * 2 + h][:LANES // 2])
            lhs[0:LANES // 2, (side * 4 + h * 2 + 1) * LANES:(side * 4 + h * 2 + 2) * LANES] = (
                sums[side * 2 + h][LANES // 2:])

    for side in range(2):
        for quarter in range(4):
            def fix(k, carry):
                r = side * 32 + quarter * 8 + k
                total = lhs[pl.ds(pl.multiple_of(k * TR, TR), TR),
                            pl.ds((side * 4 + quarter) * LANES, LANES)]
                left = faces[pl.ds(pl.multiple_of(r * TR, TR), TR), :]
                change = 0.5 * (total - counts[side] * left)
                for j in range(8):
                    at_start = change if j == 0 else pltpu.roll(change, LANES - 2 * j, 1)
                    at_middle = pltpu.roll(change, 63 - 2 * j, 1)
                    add = jnp.where(lane == 0, at_start, jnp.where(lane == 64, at_middle, 0.0))
                    out_ref[r, :, j * LANES : (j + 1) * LANES] += add
                return carry

            lax.fori_loop(0, 8, fix, 0)

    message(s, partner, 16, 0).wait_send()

    def clean_message(step, carry):
        other = (s + step) % 16
        message(other, row, 0, 2 * step).wait_send()
        message(other, partner, 16, 2 * step + 1).wait_send()
        return carry

    lax.fori_loop(1, 16, clean_message, 0)


def per_device(
    tracers, shifts, fractions, record_owner, record_source, record_parity, record_place
):
    tiled = (TR, CHUNKS, TILES, CR, LANES)
    in_tiles = jnp.transpose(tracers.reshape(TR, CHUNKS, CR, TILES, LANES), (0, 1, 3, 2, 4))
    hbm = pl.BlockSpec(memory_space=pltpu.HBM)
    f32 = jnp.float32
    dma = pltpu.SemaphoreType.DMA
    swept = pl.pallas_call(
        sweep_kernel,
        out_shape=jax.ShapeDtypeStruct((ROWS, TR, COLS), f32),
        in_specs=[hbm] * 7,
        out_specs=pl.BlockSpec(memory_space=pltpu.VMEM),
        scratch_shapes=[
            pltpu.SMEM((1, 16), jnp.int32),
            pltpu.SMEM((1, 16), jnp.int32),
            pltpu.SMEM((1, 16), jnp.int32),
            pltpu.SMEM((1, 16), jnp.int32),
            pltpu.VMEM(tiled, f32),
            pltpu.VMEM(tiled, f32),
            pltpu.VMEM(tiled, f32),
            pltpu.VMEM((WIDTH, CR, TR, LANES), f32),
            pltpu.VMEM((TR, CHUNKS - FORWARD, TILES, CR, LANES), f32),
            pltpu.VMEM((9, ROWS, LANES), jnp.int32),
            pltpu.VMEM((9, ROWS, LANES), f32),
            pltpu.VMEM((ROWS, LANES), jnp.int32),
            pltpu.SMEM((ROWS, LANES), jnp.int32),
            pltpu.VMEM((CR * TR, COLS + LANES), f32),
            pltpu.VMEM((COLS + LANES, LANES), f32),
            pltpu.VMEM((ROWS * TR, LANES), f32),
            pltpu.VMEM((LANES, LANES), f32),
            pltpu.VMEM((LANES, LANES), f32),
            pltpu.VMEM((LANES, LANES), f32),
            pltpu.VMEM((16, 8, LANES), f32),
            pltpu.VMEM((32, 8, LANES), f32),
            dma, dma((2, TILES)), dma((4,)), dma((2,)), dma((2,)), dma,
            dma((CHUNKS,)), dma((CHUNKS,)),
            dma((CHUNKS - FORWARD,)), dma((CHUNKS - FORWARD,)),
            dma((CHUNKS,)), dma((CHUNKS,)),
            dma((32,)), dma, dma,
        ],
        compiler_params=pltpu.CompilerParams(
            collective_id=0, has_side_effects=True, vmem_limit_bytes=40 << 20),
    )(
        *[pltpu.with_memory_space_constraint(v, pltpu.HBM) for v in (in_tiles, shifts, fractions, record_owner.reshape(1, 16), record_source, record_parity, record_place)]
    )
    return jnp.transpose(swept, (1, 0, 2))


def solution(mesh):
    return jax.shard_map(
        per_device,
        mesh=mesh,
        in_specs=(
            P(None, "rows", "stream"),
            P("rows", "stream"),
            P("rows", "stream"),
            P("rows", "stream", None),
            P("rows", "stream"),
            P("rows", "stream"),
            P("rows", "stream"),
        ),
        out_specs=P(None, "rows", "stream"),
        check_vma=False,
    )
```

profile of v0, /device:TPU:1, one launch (start us, length us, event | category | flops | bytes accessed | tf_op | source)
XLA Modules:
  0.0 89.1 jit_solution(12275480865842496886)
XLA Ops:
  0.0 86.6 %shard_map.73 = f32[64,8,1024]{2,1,0:T(8,128)S(1)} custom-call(f32[8,8,8,8,128]{4,3,2,1,0:T(8,128)} %bitcast.6, s32[64,1024]{1,0:T(8,128)} %shift_ref.1, f32[64,1024]{1,0:T(8,128)} %frac_ref.1, s32[1,16]{1,0:T(1,128)} %bitcast.7, s32[1,16]{1,0:T(1,128)} %source_in.1, s32[1,16]{1,0:T(1,128)} %parity_in.1, s32[1,16]{1,0:T(1,128)} %place_in.1), custom_call_target="tpu_custom_call" | custom-call | tf_op jit(solution)/shard_map/pallas_call | solution.py:359
  86.6 2.5 %copy.8 = f32[8,64,1024]{2,1,0:T(8,128)} copy(f32[8,64,1024]{2,0,1:T(8,128)S(1)} %bitcast.5) | data formatting | bytes 4194304 | tf_op jit(solution)/shard_map/transpose | solution.py:397
where the time goes:
time: 89.2 us; the launch traced here: 89.1 us
  Pallas kernels  86.6 us (97%)
  local copies, waits for them, and re-layouts  2.54 us (3%)
    pallas_call x1, Pallas kernels, per_device(): pl.pallas_call(sweep_kernel, out_shape=jax.ShapeDtypeStruct((ROWS, TR, CO...  86.6 us
    transpose x1, local copies, waits for them, and re-layouts, per_device(): return jnp.transpose(swept, (1, 0, 2))  2.54 us

commit v1 on v0

--- a/solution.py
+++ b/solution.py
@@ -18,7 +18,6 @@
 CR = ROWS // CHUNKS
 FORWARD = 5
 MESH = pl.DeviceIdType.MESH
-HIGHEST = lax.Precision.HIGHEST
 
 
 def shifted(pieces, amount):
@@ -31,11 +30,22 @@
     ]
 
 
+def times_hot(value, hot, dims):
+    high = value.astype(jnp.bfloat16)
+    rest = value - high.astype(jnp.float32)
+    middle = rest.astype(jnp.bfloat16)
+    last = (rest - middle.astype(jnp.float32)).astype(jnp.bfloat16)
+    return sum(
+        lax.dot_general(part, hot, dims, preferred_element_type=jnp.float32)
+        for part in (last, middle, high)
+    )
+
+
 def sweep_kernel(
     t_ref, shift_ref, frac_ref, owner_in, source_in, parity_in, place_in,
     out_ref,
     owner_ref, source_ref, parity_ref, place_ref, own_buf, near_buf, far_buf, work, relay_buf, shift_tile, frac_tile, least_v, least_s, lhs, ones_mat, faces,
-    hot_a, hot_b, codes, send_buf, recv_buf,
+    hots, codes, sums, send_buf, recv_buf,
     own_sem, tile_sem, record_sem, edge_send, edge_recv, least_sem,
     first_send, first_recv, middle_send, middle_recv, last_send, last_recv, msg_send, msg_recv, msg_own,
 ):
@@ -124,9 +134,10 @@
     work[1] = zero
     work[WIDTH - 1] = zero
     cell = lax.broadcasted_iota(jnp.int32, (COLS, LANES), 0)
-    face = lax.broadcasted_iota(jnp.int32, (COLS, LANES), 1)
-    ones_mat[0:COLS, :] = jnp.where(cell < face * BLOCK, 1.0, 0.0)
-    ones_mat[COLS:, :] = jnp.ones((LANES, LANES), jnp.float32)
+    face_lane = lax.broadcasted_iota(jnp.int32, (COLS, LANES), 1)
+    face = 2 * (face_lane % 64) + face_lane // 64
+    ones_mat[0:COLS, :] = jnp.where(cell < face * BLOCK, 1.0, 0.0).astype(jnp.bfloat16)
+    ones_mat[COLS:, :] = jnp.ones((LANES, LANES), jnp.bfloat16)
 
     for copy in staged:
         copy.wait()
@@ -141,13 +152,14 @@
         for i in range(j):
             earlier = earlier + jnp.where(owner_ref[0, i] == owner, 1, 0)
         at = owner * 8 + 2 * earlier
-        here = column == source_ref[0, j] + 1
+        at_face = source_ref[0, j] + 1
+        here = column == (at_face % 2) * 64 + at_face // 2
         label = (parity_ref[0, j] * 32 + place_ref[0, j] + 1).astype(jnp.float32)
         first_hot = jnp.where((slot == at) & here, 1.0, first_hot)
         second_hot = jnp.where((slot == at + 1) & here, 1.0, second_hot)
         code = jnp.where((slot == at + 4) | (slot == at + 5), label, code)
-    hot_a[...] = first_hot
-    hot_b[...] = second_hot
+    hots[0] = first_hot.astype(jnp.bfloat16)
+    hots[1] = second_hot.astype(jnp.bfloat16)
     codes[...] = code
 
     edge_s.wait_recv()
@@ -205,9 +217,24 @@
             work[PAD + TILES + j] = jnp.where(
                 s >= 1, jnp.transpose(near_buf[:, c, j], (1, 0, 2)), 0.0)
             work[OWN + j] = jnp.transpose(own_buf[:, c, j], (1, 0, 2))
-        lax.fori_loop(0, CR, one_row, c, unroll=4)
-        faces[pl.ds(pl.multiple_of(c * CR * TR, CR * TR), CR * TR), :] = jnp.dot(
-            lhs[...], ones_mat[...], precision=HIGHEST, preferred_element_type=jnp.float32)
+        lax.fori_loop(0, CR, one_row, c, unroll=8)
+        faces[pl.ds(pl.multiple_of(c * CR * TR, CR * TR), CR * TR), :] = times_hot(
+            lhs[...], ones_mat[...], (((1,), (0,)), ((), ())))
+
+    across = (((1,), (1,)), ((), ()))
+    half = ROWS // 4 * TR
+
+    def pack(h):
+        pairs = faces[2 * h * half : 2 * (h + 1) * half, :].reshape(ROWS // 4, 2, TR, LANES)
+        fine = (0.5 * (pairs[:, 0] + pairs[:, 1])).reshape(half, LANES)
+        high = fine.astype(jnp.bfloat16)
+        rest = fine - high.astype(jnp.float32)
+        middle = rest.astype(jnp.bfloat16)
+        last = (rest - middle.astype(jnp.float32)).astype(jnp.bfloat16)
+        hot = hots[h]
+        return sum(
+            lax.dot_general(hot, part, across, preferred_element_type=jnp.float32)
+            for part in (last, middle, high))
 
     def pass_on(c):
         direct(c).wait_recv()
@@ -249,20 +276,11 @@
     finish(2)
     finish(6)
     finish(3)
+    codes[...] += pack(0)
     finish(7)
     finish(4)
 
-    pairs = faces[...].reshape(ROWS // 2, 2, TR, LANES)
-    fine = (0.5 * (pairs[:, 0] + pairs[:, 1])).reshape(ROWS // 2 * TR, LANES)
-    across = (((1,), (1,)), ((), ()))
-    half = ROWS // 4 * TR
-    packed = (
-        lax.dot_general(hot_a[...], fine[:half], across, precision=HIGHEST,
-                        preferred_element_type=jnp.float32)
-        + lax.dot_general(hot_b[...], fine[half:], across, precision=HIGHEST,
-                          preferred_element_type=jnp.float32)
-        + codes[...]
-    )
+    packed = codes[...] + pack(1)
     send_buf[...] = packed.reshape(16, 8, LANES)
 
     def message(other, other_row, slot_base, k):
@@ -300,42 +318,34 @@
     received = received.reshape(2 * LANES, LANES)
     part = lax.broadcasted_iota(jnp.int32, (2 * LANES, LANES), 0) % 8
     spot = lax.broadcasted_iota(jnp.int32, (2 * LANES, LANES), 1)
+    group = spot % 64 // TILES
+    block = 2 * (spot % TILES) + spot // 64
+    wanted = jnp.where(group < 4, (row % 2) * 32 + 2 * block + group % 2 + 1, -1).astype(jnp.float32)
+    hot = jnp.where((names == wanted) & ((part == group // 2) | (part == group // 2 + 2)), 1.0, 0.0)
+    hot = hot.astype(jnp.bfloat16)
     down = (((0,), (0,)), ((), ()))
-    sums = []
-    counts = []
+    sums[...] = times_hot(received, hot, down)
+    count = jnp.dot(jnp.ones((TR, 2 * LANES), jnp.bfloat16), hot, preferred_element_type=jnp.float32)
+
     for side in range(2):
-        wanted = jnp.where(spot < 16, (row % 2) * 32 + 2 * spot + side + 1, -1).astype(jnp.float32)
-        found = names == wanted
+        count_here = count if side == 0 else pltpu.roll(count, LANES - side * TILES, 1)
         for h in range(2):
-            hot = jnp.where(found & ((part == h) | (part == h + 2)), 1.0, 0.0)
-            sums.append(lax.dot_general(received, hot, down, precision=HIGHEST,
-                                        preferred_element_type=jnp.float32))
-            if h == 0:
-                counts.append(jnp.dot(jnp.ones((8, 2 * LANES), jnp.float32), hot,
-                                      preferred_element_type=jnp.float32))
-    for side in range(2):
-        for h in range(2):
-            lhs[0:LANES // 2, (side * 4 + h * 2) * LANES:(side * 4 + h * 2 + 1) * LANES] = (
-                sums[side * 2 + h][:LANES // 2])
-            lhs[0:LANES // 2, (side * 4 + h * 2 + 1) * LANES:(side * 4 + h * 2 + 2) * LANES] = (
-                sums[side * 2 + h][LANES // 2:])
-
-    for side in range(2):
-        for quarter in range(4):
-            def fix(k, carry):
-                r = side * 32 + quarter * 8 + k
-                total = lhs[pl.ds(pl.multiple_of(k * TR, TR), TR),
-                            pl.ds((side * 4 + quarter) * LANES, LANES)]
+            base = side * 32 + h * 16
+            back = (LANES - (h * 2 + side) * TILES) % LANES
+
+            def fix(k, carry, base=base, back=back, count_here=count_here):
+                r = base + k
+                sent = sums[pl.ds(pl.multiple_of(k * TR, TR), TR), :]
+                sent = pltpu.roll(sent, back, 1) if back else sent
                 left = faces[pl.ds(pl.multiple_of(r * TR, TR), TR), :]
-                change = 0.5 * (total - counts[side] * left)
-                for j in range(8):
-                    at_start = change if j == 0 else pltpu.roll(change, LANES - 2 * j, 1)
-                    at_middle = pltpu.roll(change, 63 - 2 * j, 1)
-                    add = jnp.where(lane == 0, at_start, jnp.where(lane == 64, at_middle, 0.0))
-                    out_ref[r, :, j * LANES : (j + 1) * LANES] += add
+                change = 0.5 * (sent - count_here * left)
+                for j in range(TILES):
+                    turned = pltpu.roll(change, LANES - j, 1) if j else change
+                    out_ref[r, :, j * LANES : (j + 1) * LANES] += jnp.where(
+                        lane % 64 == 0, turned, 0.0)
                 return carry
 
-            lax.fori_loop(0, 8, fix, 0)
+            lax.fori_loop(0, 16, fix, 0, unroll=4)
 
     message(s, partner, 16, 0).wait_send()
 
@@ -376,9 +386,9 @@
             pltpu.VMEM((ROWS, LANES), jnp.int32),
             pltpu.SMEM((ROWS, LANES), jnp.int32),
             pltpu.VMEM((CR * TR, COLS + LANES), f32),
-            pltpu.VMEM((COLS + LANES, LANES), f32),
+            pltpu.VMEM((COLS + LANES, LANES), jnp.bfloat16),
             pltpu.VMEM((ROWS * TR, LANES), f32),
-            pltpu.VMEM((LANES, LANES), f32),
+            pltpu.VMEM((2, LANES, LANES), jnp.bfloat16),
             pltpu.VMEM((LANES, LANES), f32),
             pltpu.VMEM((LANES, LANES), f32),
             pltpu.VMEM((16, 8, LANES), f32),

time: 89.2 us -> 83.7 us (0.938)
  Pallas kernels: 86.6 us -> 81 us
    pallas_call x1, Pallas kernels: 86.6 us -> 81 us  [per_device(): pl.pallas_call(sweep_kernel, out_shape=jax.ShapeDtypeStruct((ROWS, TR, CO...]
where the time goes in v1:
time: 83.7 us; the launch traced here: 83.6 us
  Pallas kernels  81 us (97%)
  local copies, waits for them, and re-layouts  2.54 us (3%)
    pallas_call x1, Pallas kernels, per_device(): pl.pallas_call(sweep_kernel, out_shape=jax.ShapeDtypeStruct((ROWS, TR, CO...  81 us
    transpose x1, local copies, waits for them, and re-layouts, per_device(): return jnp.transpose(swept, (1, 0, 2))  2.54 us

profile of v1, /device:TPU:1, one launch (start us, length us, event | category | flops | bytes accessed | tf_op | source)
XLA Modules:
  0.0 83.6 jit_solution(15799536846392823575)
XLA Ops:
  0.0 81.0 %shard_map.73 = f32[64,8,1024]{2,1,0:T(8,128)S(1)} custom-call(f32[8,8,8,8,128]{4,3,2,1,0:T(8,128)} %bitcast.6, s32[64,1024]{1,0:T(8,128)} %shift_ref.1, f32[64,1024]{1,0:T(8,128)} %frac_ref.1, s32[1,16]{1,0:T(1,128)} %bitcast.7, s32[1,16]{1,0:T(1,128)} %source_in.1, s32[1,16]{1,0:T(1,128)} %parity_in.1, s32[1,16]{1,0:T(1,128)} %place_in.1), custom_call_target="tpu_custom_call" | custom-call | tf_op jit(solution)/shard_map/pallas_call | solution.py:369
  81.0 2.5 %copy.8 = f32[8,64,1024]{2,1,0:T(8,128)} copy(f32[8,64,1024]{2,0,1:T(8,128)S(1)} %bitcast.5) | data formatting | bytes 4194304 | tf_op jit(solution)/shard_map/transpose | solution.py:407

commit v2 on v1

--- a/solution.py
+++ b/solution.py
@@ -16,7 +16,12 @@
 WIDTH = OWN + TILES + 1
 CHUNKS = 8
 CR = ROWS // CHUNKS
-FORWARD = 5
+PIECES = ((0, 0, 8), (1, 0, 8), (2, 0, 8), (3, 0, 8), (4, 0, 8), (5, 0, 8), (6, 0, 8), (7, 0, 8))
+PLUS = 5
+AHEAD = 4
+AHEAD_MINUS = 3
+FAR_FIRST = (10, 9, 11, 6, 14, 2, 8, 5, 7, 13, 15, 1, 3, 4, 12)
+MINUS = len(PIECES) - PLUS
 MESH = pl.DeviceIdType.MESH
 
 
@@ -85,34 +90,33 @@
         copy.start()
     pl.semaphore_wait(barrier, 31)
 
-    def unit(ref, c):
-        return ref.at[:, c]
-
-    def direct(c):
+    def unit(ref, p):
+        block, first, many = PIECES[p]
+        return ref.at[pl.ds(first, many), block]
+
+    def parked(p):
+        _, first, many = PIECES[p]
+        return relay_buf.at[pl.ds(first, many), p - PLUS]
+
+    def send(source, target, send_sem, recv_sem, device):
         return pltpu.make_async_remote_copy(
-            unit(t_ref, c), unit(near_buf, c),
-            first_send.at[c], first_recv.at[c], device_id=after, device_id_type=MESH)
-
-    def forward(c):
-        return pltpu.make_async_remote_copy(
-            unit(near_buf, c), unit(far_buf, c),
-            last_send.at[c], last_recv.at[c], device_id=after, device_id_type=MESH)
-
-    def leg_1(c):
-        return pltpu.make_async_remote_copy(
-            unit(t_ref, c), unit(relay_buf, c - FORWARD),
-            first_send.at[c], first_recv.at[c], device_id=via, device_id_type=MESH)
-
-    def leg_2(c):
-        return pltpu.make_async_remote_copy(
-            unit(relay_buf, c - FORWARD), unit(far_buf, c),
-            middle_send.at[c - FORWARD], middle_recv.at[c - FORWARD],
-            device_id=relayed_to, device_id_type=MESH)
-
-    def leg_3(c):
-        return pltpu.make_async_remote_copy(
-            unit(far_buf, c), unit(near_buf, c),
-            last_send.at[c], last_recv.at[c], device_id=ahead, device_id_type=MESH)
+            source, target, send_sem, recv_sem, device_id=device, device_id_type=MESH)
+
+    def direct(p):
+        return send(unit(t_ref, p), unit(near_buf, p), first_send.at[p], first_recv.at[p], after)
+
+    def forward(p):
+        return send(unit(near_buf, p), unit(far_buf, p), last_send.at[p], last_recv.at[p], after)
+
+    def leg_1(p):
+        return send(unit(t_ref, p), parked(p), first_send.at[p], first_recv.at[p], via)
+
+    def leg_2(p):
+        return send(parked(p), unit(far_buf, p), middle_send.at[p - PLUS],
+                    middle_recv.at[p - PLUS], relayed_to)
+
+    def leg_3(p):
+        return send(unit(far_buf, p), unit(near_buf, p), last_send.at[p], last_recv.at[p], ahead)
 
     tail = pl.ds(COLS - LANES, LANES)
     edge_s = pltpu.make_async_remote_copy(
@@ -123,10 +127,11 @@
         device_id=after, device_id_type=MESH)
     edge_s.start()
     edge_f.start()
-    direct(0).start()
-    leg_1(FORWARD).start()
-    direct(1).start()
-    leg_1(FORWARD + 1).start()
+    for i in range(max(AHEAD, AHEAD_MINUS)):
+        if i < AHEAD:
+            direct(i).start()
+        if i < AHEAD_MINUS:
+            leg_1(PLUS + i).start()
 
     lane = lax.broadcasted_iota(jnp.int32, (TR, LANES), 1)
     zero = jnp.zeros((CR, TR, LANES), jnp.float32)
@@ -211,7 +216,9 @@
         return c
 
     def finish(c):
-        forward(c).wait_recv()
+        for p, piece in enumerate(PIECES):
+            if piece[0] == c:
+                (forward(p) if p < PLUS else leg_3(p)).wait_recv()
         for j in range(TILES):
             work[PAD + j] = jnp.where(s >= 2, jnp.transpose(far_buf[:, c, j], (1, 0, 2)), 0.0)
             work[PAD + TILES + j] = jnp.where(
@@ -236,47 +243,44 @@
             lax.dot_general(hot, part, across, preferred_element_type=jnp.float32)
             for part in (last, middle, high))
 
-    def pass_on(c):
-        direct(c).wait_recv()
-        forward(c).start()
-
-    def first_on(c):
-        leg_1(c).wait_recv()
-        leg_2(c).start()
-
-    def second_on(c):
-        leg_2(c).wait_recv()
-        leg_3(c).start()
-
-    def next_direct(c):
-        direct(c).wait_send()
-        direct(c + 2).start()
+    def pass_on(p):
+        direct(p).wait_recv()
+        forward(p).start()
+        if p + AHEAD < PLUS:
+            direct(p).wait_send()
+            direct(p + AHEAD).start()
+
+    def first_on(p):
+        leg_1(p).wait_recv()
+        leg_2(p).start()
+        if p + AHEAD_MINUS < len(PIECES):
+            leg_1(p).wait_send()
+            leg_1(p + AHEAD_MINUS).start()
+
+    def second_on(p):
+        leg_2(p).wait_recv()
+        leg_3(p).start()
 
     pass_on(0)
-    next_direct(0)
     first_on(5)
-    leg_1(5).wait_send()
-    leg_1(7).start()
     pass_on(1)
-    next_direct(1)
     first_on(6)
+    pass_on(2)
+    first_on(7)
     second_on(5)
+    pass_on(3)
+    second_on(6)
+    pass_on(4)
+    second_on(7)
     own_copy.wait()
     least_copy.wait()
-    pass_on(2)
-    next_direct(2)
-    first_on(7)
-    second_on(6)
     finish(0)
-    pass_on(3)
-    second_on(7)
     finish(1)
+    finish(2)
     finish(5)
-    pass_on(4)
-    finish(2)
-    finish(6)
     finish(3)
     codes[...] += pack(0)
+    finish(6)
     finish(7)
     finish(4)
 
@@ -298,16 +302,17 @@
         message(other, partner, 16, 2 * step + 1).start()
         return carry
 
-    lax.fori_loop(1, 16, send_out, 0)
-
-    for c in range(CHUNKS):
-        forward(c).wait_send()
-    for c in (3, 4):
-        direct(c).wait_send()
-    for c in (5, 6, 7):
-        if c != 5:
-            leg_1(c).wait_send()
-        leg_2(c).wait_send()
+    for step in FAR_FIRST:
+        send_out(step, 0)
+
+    for p in range(len(PIECES)):
+        (forward(p) if p < PLUS else leg_3(p)).wait_send()
+        if PLUS - AHEAD <= p < PLUS:
+            direct(p).wait_send()
+        if p >= PLUS:
+            leg_2(p).wait_send()
+        if p >= len(PIECES) - AHEAD_MINUS:
+            leg_1(p).wait_send()
     edge_s.wait_send()
     edge_f.wait_send()
 
@@ -345,7 +350,7 @@
                         lane % 64 == 0, turned, 0.0)
                 return carry
 
-            lax.fori_loop(0, 16, fix, 0, unroll=4)
+            lax.fori_loop(0, 16, fix, 0, unroll=16)
 
     message(s, partner, 16, 0).wait_send()
 
@@ -380,7 +385,7 @@
             pltpu.VMEM(tiled, f32),
             pltpu.VMEM(tiled, f32),
             pltpu.VMEM((WIDTH, CR, TR, LANES), f32),
-            pltpu.VMEM((TR, CHUNKS - FORWARD, TILES, CR, LANES), f32),
+            pltpu.VMEM((TR, MINUS, TILES, CR, LANES), f32),
             pltpu.VMEM((9, ROWS, LANES), jnp.int32),
             pltpu.VMEM((9, ROWS, LANES), f32),
             pltpu.VMEM((ROWS, LANES), jnp.int32),
@@ -394,9 +399,8 @@
             pltpu.VMEM((16, 8, LANES), f32),
             pltpu.VMEM((32, 8, LANES), f32),
             dma, dma((2, TILES)), dma((4,)), dma((2,)), dma((2,)), dma,
-            dma((CHUNKS,)), dma((CHUNKS,)),
-            dma((CHUNKS - FORWARD,)), dma((CHUNKS - FORWARD,)),
-            dma((CHUNKS,)), dma((CHUNKS,)),
+            dma((len(PIECES),)), dma((len(PIECES),)), dma((MINUS,)), dma((MINUS,)),
+            dma((len(PIECES),)), dma((len(PIECES),)),
             dma((32,)), dma, dma,
         ],
         compiler_params=pltpu.CompilerParams(

time: 83.7 us -> 82.4 us (0.984)
  Pallas kernels: 81 us -> 79.8 us
    pallas_call x1, Pallas kernels: 81 us -> 79.8 us  [per_device(): pl.pallas_call(sweep_kernel, out_shape=jax.ShapeDtypeStruct((ROWS, TR, CO...]
where the time goes in v2:
time: 82.4 us; the launch traced here: 82.3 us
  Pallas kernels  79.8 us (97%)
  local copies, waits for them, and re-layouts  2.54 us (3%)
    pallas_call x1, Pallas kernels, per_device(): pl.pallas_call(sweep_kernel, out_shape=jax.ShapeDtypeStruct((ROWS, TR, CO...  79.8 us
    transpose x1, local copies, waits for them, and re-layouts, per_device(): return jnp.transpose(swept, (1, 0, 2))  2.54 us

profile of v2, /device:TPU:1, one launch (start us, length us, event | category | flops | bytes accessed | tf_op | source)
XLA Modules:
  0.0 82.3 jit_solution(1648498557577550076)
XLA Ops:
  0.0 79.8 %shard_map.73 = f32[64,8,1024]{2,1,0:T(8,128)S(1)} custom-call(f32[8,8,8,8,128]{4,3,2,1,0:T(8,128)} %bitcast.6, s32[64,1024]{1,0:T(8,128)} %shift_ref.1, f32[64,1024]{1,0:T(8,128)} %frac_ref.1, s32[1,16]{1,0:T(1,128)} %bitcast.7, s32[1,16]{1,0:T(1,128)} %source_in.1, s32[1,16]{1,0:T(1,128)} %parity_in.1, s32[1,16]{1,0:T(1,128)} %place_in.1), custom_call_target="tpu_custom_call" | custom-call | tf_op jit(solution)/shard_map/pallas_call | solution.py:374
  79.8 2.5 %copy.8 = f32[8,64,1024]{2,1,0:T(8,128)} copy(f32[8,64,1024]{2,0,1:T(8,128)S(1)} %bitcast.5) | data formatting | bytes 4194304 | tf_op jit(solution)/shard_map/transpose | solution.py:411

commit v3 on v2

--- a/solution.py
+++ b/solution.py
@@ -82,7 +82,7 @@
         for i, (source, target) in enumerate(
             [(owner_in, owner_ref), (source_in, source_ref), (parity_in, parity_ref), (place_in, place_ref)])
     ] + [
-        pltpu.make_async_copy(source.at[:, pl.ds(j * LANES, LANES)], target.at[j + 1], tile_sem.at[i, j])
+        pltpu.make_async_copy(source.at[:, pl.ds(j * LANES, LANES)], target.at[j + 1, pl.ds(0, ROWS)], tile_sem.at[i, j])
         for i, (source, target) in enumerate([(shift_ref, shift_tile), (frac_ref, frac_tile)])
         for j in range(TILES)
     ]
@@ -120,10 +120,10 @@
 
     tail = pl.ds(COLS - LANES, LANES)
     edge_s = pltpu.make_async_remote_copy(
-        shift_ref.at[:, tail], shift_tile.at[0], edge_send.at[0], edge_recv.at[0],
+        shift_ref.at[:, tail], shift_tile.at[0, pl.ds(0, ROWS)], edge_send.at[0], edge_recv.at[0],
         device_id=after, device_id_type=MESH)
     edge_f = pltpu.make_async_remote_copy(
-        frac_ref.at[:, tail], frac_tile.at[0], edge_send.at[1], edge_recv.at[1],
+        frac_ref.at[:, tail], frac_tile.at[0, pl.ds(0, ROWS)], edge_send.at[1], edge_recv.at[1],
         device_id=after, device_id_type=MESH)
     edge_s.start()
     edge_f.start()
@@ -169,7 +169,7 @@
 
     edge_s.wait_recv()
     edge_f.wait_recv()
-    least = jnp.min(jnp.min(shift_tile[...], axis=0), axis=1, keepdims=True)
+    least = jnp.min(jnp.min(shift_tile[:, 0:ROWS, :], axis=0), axis=1, keepdims=True)
     least_v[...] = jnp.broadcast_to(least, (ROWS, LANES))
     least_copy = pltpu.make_async_copy(least_v, least_s, least_sem)
     least_copy.start()
@@ -386,8 +386,8 @@
             pltpu.VMEM(tiled, f32),
             pltpu.VMEM((WIDTH, CR, TR, LANES), f32),
             pltpu.VMEM((TR, MINUS, TILES, CR, LANES), f32),
-            pltpu.VMEM((9, ROWS, LANES), jnp.int32),
-            pltpu.VMEM((9, ROWS, LANES), f32),
+            pltpu.VMEM((9, ROWS + TR, LANES), jnp.int32),
+            pltpu.VMEM((9, ROWS + TR, LANES), f32),
             pltpu.VMEM((ROWS, LANES), jnp.int32),
             pltpu.SMEM((ROWS, LANES), jnp.int32),
             pltpu.VMEM((CR * TR, COLS + LANES), f32),

time: 82.4 us -> 82.4 us (level)
  no operation moved by 1% of the time
where the time goes in v3:
time: 82.4 us; the launch traced here: 82.3 us
  Pallas kernels  79.8 us (97%)
  local copies, waits for them, and re-layouts  2.54 us (3%)
    pallas_call x1, Pallas kernels, per_device(): pl.pallas_call(sweep_kernel, out_shape=jax.ShapeDtypeStruct((ROWS, TR, CO...  79.8 us
    transpose x1, local copies, waits for them, and re-layouts, per_device(): return jnp.transpose(swept, (1, 0, 2))  2.54 us

profile of v3, /device:TPU:1, one launch (start us, length us, event | category | flops | bytes accessed | tf_op | source)
XLA Modules:
  0.0 82.3 jit_solution(15354706506717314658)
XLA Ops:
  0.0 79.8 %shard_map.73 = f32[64,8,1024]{2,1,0:T(8,128)S(1)} custom-call(f32[8,8,8,8,128]{4,3,2,1,0:T(8,128)} %bitcast.6, s32[64,1024]{1,0:T(8,128)} %shift_ref.1, f32[64,1024]{1,0:T(8,128)} %frac_ref.1, s32[1,16]{1,0:T(1,128)} %bitcast.7, s32[1,16]{1,0:T(1,128)} %source_in.1, s32[1,16]{1,0:T(1,128)} %parity_in.1, s32[1,16]{1,0:T(1,128)} %place_in.1), custom_call_target="tpu_custom_call" | custom-call | tf_op jit(solution)/shard_map/pallas_call | solution.py:374
  79.8 2.5 %copy.8 = f32[8,64,1024]{2,1,0:T(8,128)} copy(f32[8,64,1024]{2,0,1:T(8,128)S(1)} %bitcast.5) | data formatting | bytes 4194304 | tf_op jit(solution)/shard_map/transpose | solution.py:411
